TPU v7x, 256 devices: a whole 4x4x8 slice. The times are simulated.
256 devices in a mesh: leaf: 256 (over y, z, x, core).
Axes of the slice: x: 4, y: 4, z: 8, core: 2. Of those that a mesh axis runs over, the one named last changes fastest.
Arguments:
- fields: bfloat16 [524288, 128], P('leaf'), may hold values from -6 to 6
- in_basis: bfloat16 [524288, 128], P('leaf'), may hold values from -0.375 to 0.375
- out_basis: bfloat16 [524288, 128], P('leaf'), may hold values from -0.5 to 0.5
- couplings: bfloat16 [11, 2048, 2, 128, 128], P(None, 'leaf'), may hold values from -0.375 to 0.375
- near_blocks: bfloat16 [2048, 3, 256, 256], P('leaf'), may hold values from -0.21875 to 0.21875
Outputs:
- scattered: bfloat16 [524288, 128], P('leaf')
All inputs are finite; a program needn't handle non-finite values.
Results may differ from a plain program's by a relative error of at most 0.015.
Values may be sent and summed in bfloat16 or wider, within the bound.
A program may use at most 64 MiB of HBM per device.

v0:
```python
import jax
import jax.numpy as jnp
from jax import lax
from jax.sharding import PartitionSpec as P


def from_partner(block, axis, stride):
    count = lax.axis_size(axis)
    route = []
    for low in range(count):
        high = low | 1 << stride
        if high != low and high < count:
            route += [(low, high), (high, low)]
    return lax.ppermute(block, axis, route)


def padded_2(block, sides, width):
    for axis, dim in sides:
        count = lax.axis_size(axis)
        forward = [(i, i + 1) for i in range(count - 1)]
        backward = [(target, source) for source, target in forward]
        low = lax.ppermute(
            lax.slice_in_dim(block, block.shape[dim] - width, None, axis=dim), axis, forward
        )
        high = lax.ppermute(lax.slice_in_dim(block, 0, width, axis=dim), axis, backward)
        block = jnp.concatenate([low, block, high], axis=dim)
    return block


def local_level(coeffs, mixing, bit_pos):
    leaf_count = coeffs.shape[0]
    stride = 2**bit_pos
    grouped = coeffs.reshape(
        leaf_count // (2 * stride), 2, stride, coeffs.shape[1], coeffs.shape[2]
    )
    low_half = jnp.broadcast_to(grouped[:, 0:1], grouped.shape).reshape(coeffs.shape)
    high_half = jnp.broadcast_to(grouped[:, 1:2], grouped.shape).reshape(coeffs.shape)
    summed = jnp.einsum("bij,bjc->bic", mixing[:, 0], low_half, preferred_element_type=jnp.float32)
    summed = summed + jnp.einsum(
        "bij,bjc->bic", mixing[:, 1], high_half, preferred_element_type=jnp.float32
    )
    return summed.astype(jnp.bfloat16)


def cross_term(mixing, coeffs, which_side):
    chosen = lax.dynamic_index_in_dim(mixing, which_side, 1, False)
    return jnp.einsum("bij,bjc->bic", chosen, coeffs, preferred_element_type=jnp.float32)


def per_device(fields, in_basis, out_basis, couplings, near_blocks):
    leaf_count = near_blocks.shape[0]
    leaf_rows = near_blocks.shape[2]
    rhs_width = fields.shape[1]
    rank_width = in_basis.shape[1]
    blocks = fields.reshape(leaf_count, leaf_rows, rhs_width)
    basis_in = in_basis.reshape(leaf_count, leaf_rows, rank_width)
    coeffs = jnp.einsum(
        "bmr,bmc->brc", basis_in, blocks, preferred_element_type=jnp.float32
    ).astype(jnp.bfloat16)
    local_bits = leaf_count.bit_length() - 1
    for bit_pos in range(local_bits):
        coeffs = local_level(coeffs, couplings[bit_pos], bit_pos)
    dev_bits = lax.axis_size("leaf").bit_length() - 1
    position = lax.axis_index("leaf")
    for step_bit in range(dev_bits):
        mixing = couplings[local_bits + step_bit]
        own_side = position >> step_bit & 1
        partner = from_partner(coeffs, "leaf", step_bit)
        own_term = cross_term(mixing, coeffs, own_side)
        coeffs = (own_term + cross_term(mixing, partner, 1 - own_side)).astype(jnp.bfloat16)
    basis_out = out_basis.reshape(leaf_count, leaf_rows, rank_width)
    summed = jnp.einsum("bmr,brc->bmc", basis_out, coeffs, preferred_element_type=jnp.float32)
    padded = padded_2(blocks, (("leaf", 0),), 1)
    for offset in range(3):
        summed = summed + jnp.einsum(
            "bmn,bnc->bmc",
            near_blocks[:, offset],
            padded[offset : offset + leaf_count],
            preferred_element_type=jnp.float32,
        )
    return summed.reshape(leaf_count * leaf_rows, rhs_width).astype(jnp.bfloat16)


def solution(mesh):
    placed = (
        P("leaf", None),
        P("leaf", None),
        P("leaf", None),
        P(None, "leaf", None, None, None),
        P("leaf", None, None, None),
    )
    return jax.shard_map(
        per_device, mesh=mesh, in_specs=placed, out_specs=P("leaf", None), check_vma=False
    )
```

profile of v0, /device:TPU:8, one launch (start us, length us, event | category | flops | bytes accessed | tf_op | source)
XLA Modules:
  0.0 105.4 jit_solution(623194609867015458)
XLA Ops:
  0.0 5.9 %fusion.91 = (bf16[1,8,2,128,128]{4,3,2,1,0:T(8,128)(2,1)}, bf16[1,8,2,128,128]{4,3,2,1,0:T(8,128)(2,1)}, bf16[1,8,2,128,128]{4,3,2,1,0:T(8,128)(2,1)S(1)}, bf16...) fusion(bf16[11,8,2,128,128]{4,3,2,1,0:T(8,128)(2,1)} %param.8), kind=kLoop, calls=%fused_computation.118 | loop fusion | bytes 11534336 | tf_op jit(solution)/shard_map/slice | solution.py:66
  7.5 1.3 %fusion.29 = f32[8,128,128]{2,1,0:T(8,128)S(1)} fusion(bf16[8,128,128]{1,2,0:T(8,128)(2,1)S(1)} %bitcast.169, bf16[8,2,128,128]{3,2,0,1:T(8,128)(2,1)} %bitcast.159), kind=kOutput, calls=%fused_computation.53 | convolution fusion | flops 33554432 | bytes 1048576 | tf_op jit(solution)/shard_map/bij,bjc->bic/dot_general | solution.py:38
  8.8 1.3 %fusion.3 = bf16[8,128,128]{2,1,0:T(8,128)(2,1)S(1)} fusion(f32[8,128,128]{2,1,0:T(8,128)S(1)} %fusion.29, bf16[8,128,128]{1,2,0:T(8,128)(2,1)S(1)} %bitcast.163, bf16[8,2,128,128]{3,2,0,1:T(8,128)(2,1)} %bitcast.160), kind=kOutput, calls=%fused_computation.17 | convolution fusion | flops 33816576 | bytes 1310720 | tf_op jit(solution)/shard_map/bij,bjc->bic/dot_general | solution.py:39
  11.8 1.3 %fusion.39 = f32[8,128,128]{2,1,0:T(8,128)S(1)} fusion(bf16[8,128,128]{2,1,0:T(8,128)(2,1)S(1)} %fusion.5, bf16[1,8,2,128,128]{4,3,2,1,0:T(8,128)(2,1)} %get-tuple-element.14, s32[]{:T(128)S(6)} %select_n.56), kind=kOutput, calls=%fused_computation.62 | convolution fusion | flops 33554432 | bytes 1048580 | tf_op jit(solution)/shard_map/bij,bjc->bic/dot_general | solution.py:47
  13.4 1.3 %fusion.6 = bf16[8,128,128]{2,1,0:T(8,128)(2,1)S(1)} fusion(f32[8,128,128]{2,1,0:T(8,128)S(1)} %fusion.39, bf16[8,128,128]{1,2,0:T(8,128)(2,1)} %collective-permute-done, bf16[1,8,2,128,128]{4,3,2,1,0:T(8,128)(2,1)} %get-tuple-element.14, s32[]{:T(128)S(6)} %select_n.57), kind=kOutput, calls=%fused_computation.20 | convolution fusion | flops 33816576 | bytes 1310724 | tf_op jit(solution)/shard_map/bij,bjc->bic/dot_general | solution.py:47
  14.8 1.6 %collective-permute-start.1 = (bf16[8,128,128]{2,1,0:T(8,128)(2,1)S(1)}, bf16[8,128,128]{2,1,0:T(8,128)(2,1)}, u32[]{:S(2)}, u32[]{:S(2)}) collective-permute-start(bf16[8,128,128]{2,1,0:T(8,128)(2,1)S(1)} %fusion.6), channel_id=1, source_target_pairs={{0,2},{2,0},{1,3},{3,1},{4,6},{6,4},{5,7},{7,5},{8,10},{10,8},{9,1... | collective-permute-start | bytes 786440 | tf_op jit(solution)/shard_map/ppermute | solution.py:14
  17.5 5.8 %collective-permute-done.1 = bf16[8,128,128]{2,1,0:T(8,128)(2,1)} collective-permute-done((bf16[8,128,128]{2,1,0:T(8,128)(2,1)S(1)}, bf16[8,128,128]{2,1,0:T(8,128)(2,1)}, u32[]{:S(2)}, u32[]{:S(2)}) %collective-permute-start.1) | collective-permute-done | bytes 262176 | tf_op jit(solution)/shard_map/ppermute | solution.py:14
  23.3 1.2 %fusion.7 = bf16[8,128,128]{2,1,0:T(8,128)(2,1)S(1)} fusion(f32[8,128,128]{2,1,0:T(8,128)S(1)} %fusion.41, bf16[8,128,128]{2,1,0:T(8,128)(2,1)} %collective-permute-done.1, bf16[1,8,2,128,128]{4,3,2,1,0:T(8,128)(2,1)} %get-tuple-element.8, s32[]{:T(128)S(6)} %select_n.58), kind=kOutput, calls=%fused_computation.21 | convolution fusion | flops 33816576 | bytes 1310724 | tf_op jit(solution)/shard_map/bij,bjc->bic/dot_general | solution.py:47
  24.6 3.1 %collective-permute-start.2 = (bf16[8,128,128]{2,1,0:T(8,128)(2,1)S(1)}, bf16[8,128,128]{2,1,0:T(8,128)(2,1)}, u32[]{:S(2)}, u32[]{:S(2)}) collective-permute-start(bf16[8,128,128]{2,1,0:T(8,128)(2,1)S(1)} %fusion.7), channel_id=1, source_target_pairs={{0,4},{4,0},{1,5},{5,1},{2,6},{6,2},{3,7},{7,3},{8,12},{12,8},{9,1... | collective-permute-start | bytes 786440 | tf_op jit(solution)/shard_map/ppermute | solution.py:14
  28.8 4.9 %collective-permute-done.2 = bf16[8,128,128]{2,1,0:T(8,128)(2,1)} collective-permute-done((bf16[8,128,128]{2,1,0:T(8,128)(2,1)S(1)}, bf16[8,128,128]{2,1,0:T(8,128)(2,1)}, u32[]{:S(2)}, u32[]{:S(2)}) %collective-permute-start.2) | collective-permute-done | bytes 262176 | tf_op jit(solution)/shard_map/ppermute | solution.py:14
  33.8 1.2 %fusion.8 = bf16[8,128,128]{2,1,0:T(8,128)(2,1)S(1)} fusion(f32[8,128,128]{2,1,0:T(8,128)S(1)} %fusion.43, bf16[8,128,128]{2,1,0:T(8,128)(2,1)} %collective-permute-done.2, bf16[1,8,2,128,128]{4,3,2,1,0:T(8,128)(2,1)} %get-tuple-element.9, s32[]{:T(128)S(6)} %select_n.59), kind=kOutput, calls=%fused_computation.22 | convolution fusion | flops 33816576 | bytes 1310724 | tf_op jit(solution)/shard_map/bij,bjc->bic/dot_general | solution.py:47
  35.0 2.0 %collective-permute-start.3 = (bf16[8,128,128]{2,1,0:T(8,128)(2,1)S(1)}, bf16[8,128,128]{2,1,0:T(8,128)(2,1)}, u32[]{:S(2)}, u32[]{:S(2)}) collective-permute-start(bf16[8,128,128]{2,1,0:T(8,128)(2,1)S(1)} %fusion.8), channel_id=1, source_target_pairs={{0,8},{8,0},{1,9},{9,1},{2,10},{10,2},{3,11},{11,3},{4,12},{12,4},... | collective-permute-start | bytes 786440 | tf_op jit(solution)/shard_map/ppermute | solution.py:14
  37.3 4.7 %collective-permute-done.3 = bf16[8,128,128]{2,1,0:T(8,128)(2,1)} collective-permute-done((bf16[8,128,128]{2,1,0:T(8,128)(2,1)S(1)}, bf16[8,128,128]{2,1,0:T(8,128)(2,1)}, u32[]{:S(2)}, u32[]{:S(2)}) %collective-permute-start.3) | collective-permute-done | bytes 262176 | tf_op jit(solution)/shard_map/ppermute | solution.py:14
  42.0 1.2 %fusion.9 = bf16[8,128,128]{2,1,0:T(8,128)(2,1)S(1)} fusion(f32[8,128,128]{2,1,0:T(8,128)S(1)} %fusion.45, bf16[8,128,128]{2,1,0:T(8,128)(2,1)} %collective-permute-done.3, bf16[1,8,2,128,128]{4,3,2,1,0:T(8,128)(2,1)S(1)} %get-tuple-element.10, s32[]{:T(128)S(6)} %select_n.60), kind=kOutput, calls=%fused_computation.23 | convolution fusion | flops 33816576 | bytes 1310724 | tf_op jit(solution)/shard_map/bij,bjc->bic/dot_general | solution.py:47
  43.2 3.3 %collective-permute-start.4 = (bf16[8,128,128]{2,1,0:T(8,128)(2,1)S(1)}, bf16[8,128,128]{2,1,0:T(8,128)(2,1)}, u32[]{:S(2)}, u32[]{:S(2)}) collective-permute-start(bf16[8,128,128]{2,1,0:T(8,128)(2,1)S(1)} %fusion.9), channel_id=1, source_target_pairs={{0,16},{16,0},{1,17},{17,1},{2,18},{18,2},{3,19},{19,3},{4,20},{20... | collective-permute-start | bytes 786440 | tf_op jit(solution)/shard_map/ppermute | solution.py:14
  46.7 9.6 %collective-permute-done.4 = bf16[8,128,128]{2,1,0:T(8,128)(2,1)} collective-permute-done((bf16[8,128,128]{2,1,0:T(8,128)(2,1)S(1)}, bf16[8,128,128]{2,1,0:T(8,128)(2,1)}, u32[]{:S(2)}, u32[]{:S(2)}) %collective-permute-start.4) | collective-permute-done | bytes 262176 | tf_op jit(solution)/shard_map/ppermute | solution.py:14
  57.5 6.3 %collective-permute-start.5 = (bf16[8,128,128]{2,1,0:T(8,128)(2,1)S(1)}, bf16[8,128,128]{2,1,0:T(8,128)(2,1)}, u32[]{:S(2)}, u32[]{:S(2)}) collective-permute-start(bf16[8,128,128]{2,1,0:T(8,128)(2,1)S(1)} %fusion.10), channel_id=1, source_target_pairs={{0,32},{32,0},{1,33},{33,1},{2,34},{34,2},{3,35},{35,3},{4,36},{36... | collective-permute-start | bytes 786440 | tf_op jit(solution)/shard_map/ppermute | solution.py:14
  64.1 11.4 %collective-permute-done.5 = bf16[8,128,128]{2,1,0:T(8,128)(2,1)} collective-permute-done((bf16[8,128,128]{2,1,0:T(8,128)(2,1)S(1)}, bf16[8,128,128]{2,1,0:T(8,128)(2,1)}, u32[]{:S(2)}, u32[]{:S(2)}) %collective-permute-start.5) | collective-permute-done | bytes 262176 | tf_op jit(solution)/shard_map/ppermute | solution.py:14
  77.6 6.0 %collective-permute-done.6 = bf16[8,128,128]{2,1,0:T(8,128)(2,1)S(1)} collective-permute-done((bf16[8,128,128]{2,1,0:T(8,128)(2,1)S(1)}, bf16[8,128,128]{2,1,0:T(8,128)(2,1)S(1)}, u32[]{:S(2)}, u32[]{:S(2)}) %collective-permute-start.6) | collective-permute-done | bytes 262176 | tf_op jit(solution)/shard_map/ppermute | solution.py:14
  83.8 4.4 %collective-permute-start.7 = (bf16[8,128,128]{2,1,0:T(8,128)(2,1)S(1)}, bf16[8,128,128]{2,1,0:T(8,128)(2,1)S(1)}, u32[]{:S(2)}, u32[]{:S(2)}) collective-permute-start(bf16[8,128,128]{2,1,0:T(8,128)(2,1)S(1)} %fusion.12), channel_id=1, source_target_pairs={{0,128},{128,0},{1,129},{129,1},{2,130},{130,2},{3,131},{131,3},{4... | collective-permute-start | bytes 786440 | tf_op jit(solution)/shard_map/ppermute | solution.py:14
  88.3 1.9 %collective-permute-start.8 = (bf16[1,256,128]{1,2,0:T(8,128)(2,1)S(1)}, bf16[1,256,128]{1,2,0:T(8,128)(2,1)}, u32[]{:S(2)}, u32[]{:S(2)}) collective-permute-start(bf16[1,256,128]{1,2,0:T(8,128)(2,1)S(1)} %bitcast.173), channel_id=1, source_target_pairs={{0,1},{1,2},{2,3},{3,4},{4,5},{5,6},{6,7},{7,8},{8,9},{9,10},{10,1... | collective-permute-start | bytes 196616 | tf_op jit(solution)/shard_map/ppermute | solution.py:22
  90.3 7.9 %collective-permute-start.9 = (bf16[1,256,128]{1,2,0:T(8,128)(2,1)S(1)}, bf16[1,256,128]{1,2,0:T(8,128)(2,1)S(1)}, u32[]{:S(2)}, u32[]{:S(2)}) collective-permute-start(bf16[1,256,128]{1,2,0:T(8,128)(2,1)S(1)} %bitcast.172), channel_id=1, source_target_pairs={{1,0},{2,1},{3,2},{4,3},{5,4},{6,5},{7,6},{8,7},{9,8},{10,9},{11,1... | collective-permute-start | bytes 196616 | tf_op jit(solution)/shard_map/ppermute | solution.py:25
  98.8 1.5 %fusion.14 = f32[8,128,256]{2,1,0:T(8,128)} fusion(bf16[8,256,128]{2,1,0:T(8,128)(2,1)S(1)} %bitcast.155, f32[8,128,128]{1,2,0:T(8,128)S(1)} %fusion.53, bf16[8,128,128]{2,1,0:T(8,128)(2,1)S(1)} %collective-permute-done.7, bf16[1,8,2,128,128]{4,3,2,1,0:T(8,128)(2,1)S(1)} %copy-done.4, s32[]{:T(128)S(6)} %select_n.64), kind=kOutput, calls=%fused_computation.29 | convolution fusion | flops 100925440 | bytes 2621444 | tf_op jit(solution)/shard_map/bmr,brc->bmc/dot_general | solution.py:72
  100.3 2.2 %fusion.1 = f32[8,256,128]{1,2,0:T(8,128)S(1)} fusion(f32[8,128,256]{2,1,0:T(8,128)} %fusion.14, bf16[8,3,256,256]{3,2,1,0:T(8,128)(2,1)} %param.9, bf16[8,256,128]{1,2,0:T(8,128)(2,1)S(1)} %copy.29, bf16[1,256,128]{1,2,0:T(8,128)(2,1)} %collective-permute-done.8), kind=kOutput, calls=%fused_computation.4 | convolution fusion | flops 135659520 | bytes 3735552 | tf_op jit(solution)/shard_map/bmn,bnc->bmc/dot_general | solution.py:75
  (59 shorter events, 13.6 us)
Async XLA Ops:
  0.0 98.8 %copy-start = (bf16[2048,128]{1,0:T(8,128)(2,1)S(1)}, bf16[2048,128]{1,0:T(8,128)(2,1)}, u32[]{:S(2)}) copy-start(bf16[2048,128]{1,0:T(8,128)(2,1)} %param.7) | copy-start | bytes 1572868
  0.0 6.7 %copy-start.1 = (bf16[2048,128]{1,0:T(8,128)(2,1)S(1)}, bf16[2048,128]{1,0:T(8,128)(2,1)}, u32[]{:S(2)}) copy-start(bf16[2048,128]{1,0:T(8,128)(2,1)} %param.5) | copy-start | bytes 1572868
  0.0 6.7 %copy-start.5 = (bf16[2048,128]{1,0:T(8,128)(2,1)S(1)}, bf16[2048,128]{1,0:T(8,128)(2,1)}, u32[]{:S(2)}) copy-start(bf16[2048,128]{1,0:T(8,128)(2,1)} %param.6) | copy-start | bytes 1572868
  7.4 2.7 %copy-start.2 = (bf16[1,8,2,128,128]{4,3,2,1,0:T(8,128)(2,1)S(1)}, bf16[1,8,2,128,128]{4,3,2,1,0:T(8,128)(2,1)}, u32[]{:S(2)}) copy-start(bf16[1,8,2,128,128]{4,3,2,1,0:T(8,128)(2,1)} %get-tuple-element.6) | copy-start | bytes 1572868
  7.4 2.7 %copy-start.3 = (bf16[1,8,2,128,128]{4,3,2,1,0:T(8,128)(2,1)S(1)}, bf16[1,8,2,128,128]{4,3,2,1,0:T(8,128)(2,1)}, u32[]{:S(2)}) copy-start(bf16[1,8,2,128,128]{4,3,2,1,0:T(8,128)(2,1)} %get-tuple-element.15) | copy-start | bytes 1572868
  11.7 1.8 %collective-permute-start = (bf16[8,128,128]{1,2,0:T(8,128)(2,1)S(1)}, bf16[8,128,128]{1,2,0:T(8,128)(2,1)}, u32[]{:S(2)}, u32[]{:S(2)}) collective-permute-start(bf16[8,128,128]{1,2,0:T(8,128)(2,1)S(1)} %bitcast.167), channel_id=1, source_target_pairs={{0,1},{1,0},{2,3},{3,2},{4,5},{5,4},{6,7},{7,6},{8,9},{9,8},{10,11... | collective-permute-start | bytes 786440 | tf_op jit(solution)/shard_map/ppermute | solution.py:14
  14.8 8.5 %collective-permute-start.1 = (bf16[8,128,128]{2,1,0:T(8,128)(2,1)S(1)}, bf16[8,128,128]{2,1,0:T(8,128)(2,1)}, u32[]{:S(2)}, u32[]{:S(2)}) collective-permute-start(bf16[8,128,128]{2,1,0:T(8,128)(2,1)S(1)} %fusion.6), channel_id=1, source_target_pairs={{0,2},{2,0},{1,3},{3,1},{4,6},{6,4},{5,7},{7,5},{8,10},{10,8},{9,1... | collective-permute-start | bytes 786440 | tf_op jit(solution)/shard_map/ppermute | solution.py:14
  24.6 9.2 %collective-permute-start.2 = (bf16[8,128,128]{2,1,0:T(8,128)(2,1)S(1)}, bf16[8,128,128]{2,1,0:T(8,128)(2,1)}, u32[]{:S(2)}, u32[]{:S(2)}) collective-permute-start(bf16[8,128,128]{2,1,0:T(8,128)(2,1)S(1)} %fusion.7), channel_id=1, source_target_pairs={{0,4},{4,0},{1,5},{5,1},{2,6},{6,2},{3,7},{7,3},{8,12},{12,8},{9,1... | collective-permute-start | bytes 786440 | tf_op jit(solution)/shard_map/ppermute | solution.py:14
  35.0 7.0 %collective-permute-start.3 = (bf16[8,128,128]{2,1,0:T(8,128)(2,1)S(1)}, bf16[8,128,128]{2,1,0:T(8,128)(2,1)}, u32[]{:S(2)}, u32[]{:S(2)}) collective-permute-start(bf16[8,128,128]{2,1,0:T(8,128)(2,1)S(1)} %fusion.8), channel_id=1, source_target_pairs={{0,8},{8,0},{1,9},{9,1},{2,10},{10,2},{3,11},{11,3},{4,12},{12,4},... | collective-permute-start | bytes 786440 | tf_op jit(solution)/shard_map/ppermute | solution.py:14
  43.2 13.2 %collective-permute-start.4 = (bf16[8,128,128]{2,1,0:T(8,128)(2,1)S(1)}, bf16[8,128,128]{2,1,0:T(8,128)(2,1)}, u32[]{:S(2)}, u32[]{:S(2)}) collective-permute-start(bf16[8,128,128]{2,1,0:T(8,128)(2,1)S(1)} %fusion.9), channel_id=1, source_target_pairs={{0,16},{16,0},{1,17},{17,1},{2,18},{18,2},{3,19},{19,3},{4,20},{20... | collective-permute-start | bytes 786440 | tf_op jit(solution)/shard_map/ppermute | solution.py:14
  57.5 17.9 %collective-permute-start.5 = (bf16[8,128,128]{2,1,0:T(8,128)(2,1)S(1)}, bf16[8,128,128]{2,1,0:T(8,128)(2,1)}, u32[]{:S(2)}, u32[]{:S(2)}) collective-permute-start(bf16[8,128,128]{2,1,0:T(8,128)(2,1)S(1)} %fusion.10), channel_id=1, source_target_pairs={{0,32},{32,0},{1,33},{33,1},{2,34},{34,2},{3,35},{35,3},{4,36},{36... | collective-permute-start | bytes 786440 | tf_op jit(solution)/shard_map/ppermute | solution.py:14
  63.8 34.6 %copy-start.4 = (bf16[1,8,2,128,128]{4,3,2,1,0:T(8,128)(2,1)S(1)}, bf16[1,8,2,128,128]{4,3,2,1,0:T(8,128)(2,1)}, u32[]{:S(2)}) copy-start(bf16[1,8,2,128,128]{4,3,2,1,0:T(8,128)(2,1)} %get-tuple-element.5) | copy-start | bytes 1572868
  76.6 6.9 %collective-permute-start.6 = (bf16[8,128,128]{2,1,0:T(8,128)(2,1)S(1)}, bf16[8,128,128]{2,1,0:T(8,128)(2,1)S(1)}, u32[]{:S(2)}, u32[]{:S(2)}) collective-permute-start(bf16[8,128,128]{2,1,0:T(8,128)(2,1)S(1)} %fusion.11), channel_id=1, source_target_pairs={{0,64},{64,0},{1,65},{65,1},{2,66},{66,2},{3,67},{67,3},{4,68},{68... | collective-permute-start | bytes 786440 | tf_op jit(solution)/shard_map/ppermute | solution.py:14
  83.8 15.0 %collective-permute-start.7 = (bf16[8,128,128]{2,1,0:T(8,128)(2,1)S(1)}, bf16[8,128,128]{2,1,0:T(8,128)(2,1)S(1)}, u32[]{:S(2)}, u32[]{:S(2)}) collective-permute-start(bf16[8,128,128]{2,1,0:T(8,128)(2,1)S(1)} %fusion.12), channel_id=1, source_target_pairs={{0,128},{128,0},{1,129},{129,1},{2,130},{130,2},{3,131},{131,3},{4... | collective-permute-start | bytes 786440 | tf_op jit(solution)/shard_map/ppermute | solution.py:14
  88.3 12.0 %collective-permute-start.8 = (bf16[1,256,128]{1,2,0:T(8,128)(2,1)S(1)}, bf16[1,256,128]{1,2,0:T(8,128)(2,1)}, u32[]{:S(2)}, u32[]{:S(2)}) collective-permute-start(bf16[1,256,128]{1,2,0:T(8,128)(2,1)S(1)} %bitcast.173), channel_id=1, source_target_pairs={{0,1},{1,2},{2,3},{3,4},{4,5},{5,6},{6,7},{7,8},{8,9},{9,10},{10,1... | collective-permute-start | bytes 196616 | tf_op jit(solution)/shard_map/ppermute | solution.py:22
  90.3 13.0 %collective-permute-start.9 = (bf16[1,256,128]{1,2,0:T(8,128)(2,1)S(1)}, bf16[1,256,128]{1,2,0:T(8,128)(2,1)S(1)}, u32[]{:S(2)}, u32[]{:S(2)}) collective-permute-start(bf16[1,256,128]{1,2,0:T(8,128)(2,1)S(1)} %bitcast.172), channel_id=1, source_target_pairs={{1,0},{2,1},{3,2},{4,3},{5,4},{6,5},{7,6},{8,7},{9,8},{10,9},{11,1... | collective-permute-start | bytes 196616 | tf_op jit(solution)/shard_map/ppermute | solution.py:25
  98.4 1.9 %copy-start.6 = (bf16[8,256,128]{1,2,0:T(8,128)(2,1)}, bf16[8,256,128]{1,2,0:T(8,128)(2,1)S(1)}, u32[]{:S(2)}) copy-start(bf16[8,256,128]{1,2,0:T(8,128)(2,1)S(1)} %copy.29) | copy-start | bytes 1572868
  100.3 2.6 %copy-start.8 = (bf16[8,3,256,256]{3,2,1,0:T(8,128)(2,1)S(1)}, bf16[8,3,256,256]{3,2,1,0:T(8,128)(2,1)}, u32[]{:S(2)}) copy-start(bf16[8,3,256,256]{3,2,1,0:T(8,128)(2,1)} %param.9) | copy-start | bytes 9437188
  102.8 1.0 copy-start.7
where the time goes:
time: 106 us; the launch traced here: 105 us
  waiting for transfers between devices  42.8 us (40%)
  starting transfers between devices  31.4 us (30%)
  matrix products  21.1 us (20%)
  local copies, waits for them, and re-layouts  9.69 us (9%)
    ppermute x8, waiting for transfers between devices, from_partner(): return lax.ppermute(block, axis, route)  42.8 us
    ppermute x8, starting transfers between devices, from_partner(): return lax.ppermute(block, axis, route)  21.6 us
    dot_general x15, matrix products, cross_term(): jnp.einsum('bij,bjc->bic', chosen, coeffs, preferred_element_type=jnp.flo...  12.3 us
    ppermute x1, starting transfers between devices, padded_2(): lax.ppermute(lax.slice_in_dim(block, 0, width, axis=dim), axis, backward)  7.86 us
    slice x1, local copies, waits for them, and re-layouts, per_device(): mixing = couplings[local_bits + step_bit]  5.89 us
    dot_general x3, matrix products, per_device(): jnp.einsum('bmn,bnc->bmc', near_blocks[:, offset], padded[offset:offset +...  3.17 us
  transfers between devices with their start and end apart: 10, of which 7 were waited for; matrix products, arithmetic and copies ran while one was open for 9% of the time, Pallas kernels for 0%

commit v1 on v0

v1 whole, which is shorter than its diff:
```python
import functools

import jax
import jax.numpy as jnp
from jax import lax
from jax.experimental import pallas as pl
from jax.experimental.pallas import tpu as pltpu
from jax.sharding import PartitionSpec as P

MESH = pl.DeviceIdType.MESH
F32 = jnp.float32
BF16 = jnp.bfloat16


def event_order(leaves, dev_bits):
    cost = [
        (0.9, 0.10, "c"),
        (1.7, 0.70, "x"),
        (2.4, 0.70, "x"),
        (1.7, 0.35, "z"),
        (2.4, 1.40, "z"),
        (4.0, 1.40, "z"),
        (1.7, 0.70, "y"),
        (2.4, 0.70, "y"),
    ]
    cost = [cost[level % len(cost)] for level in range(dev_bits)]
    busy = {}
    core = 0.0
    queue = []
    for leaf in range(leaves):
        core += 0.15
        start = max(core, busy.get(cost[0][2], 0.0))
        busy[cost[0][2]] = start + cost[0][1]
        queue.append((start + cost[0][1] + cost[0][0], 0, leaf))
    order = []
    while queue:
        queue.sort()
        ready, level, leaf = queue.pop(0)
        order.append((max(ready, core), level, leaf))
        core = max(ready, core) + 0.15
        if level + 1 < dev_bits:
            flight, wire, row = cost[level + 1]
            start = max(core, busy.get(row, 0.0))
            busy[row] = start + wire
            queue.append((start + wire + flight, level + 1, leaf))
    return order


def kernel(
    count,
    fields_hbm,
    in_hbm,
    out_hbm,
    coup_hbm,
    near_hbm,
    result_hbm,
    fields,
    basis_in,
    basis_out,
    coup,
    near,
    local,
    cross,
    final,
    summed,
    result,
    load_sem,
    coup_sem,
    near_sem,
    basis_sem,
    store_sem,
    halo_send,
    halo_recv,
    send_sem,
    recv_sem,
):
    leaves = near.shape[0]
    rows = near.shape[2]
    rank = basis_in.shape[1]
    levels = coup.shape[0]
    dev_bits = cross.shape[0]
    local_bits = levels - dev_bits
    me = lax.axis_index("leaf")
    right = lax.rem(me + 1, count)
    left = lax.rem(me + count - 1, count)
    sides = [lax.rem(lax.div(me, 1 << k), 2) for k in range(dev_bits)]
    partners = [me + (1 << k) * (1 - 2 * sides[k]) for k in range(dev_bits)]

    pair_rows = 2 * rows
    loads = []
    for pair in range(leaves // 2):
        at = pl.ds(pair * pair_rows, pair_rows)
        to = pl.ds(rows + pair * pair_rows, pair_rows)
        loads.append(
            (
                pltpu.make_async_copy(fields_hbm.at[at], fields.at[to], load_sem.at[0, pair]),
                pltpu.make_async_copy(in_hbm.at[at], basis_in.at[at], load_sem.at[1, pair]),
            )
        )
    coup_loads = [
        pltpu.make_async_copy(coup_hbm.at[q], coup.at[q], coup_sem.at[q]) for q in range(levels)
    ]
    near_loads = [
        pltpu.make_async_copy(near_hbm.at[b], near.at[b], near_sem.at[b]) for b in range(leaves)
    ]
    basis_load = pltpu.make_async_copy(out_hbm, basis_out, basis_sem)

    for pair in loads:
        for load in pair:
            load.start()
    for q in range(local_bits):
        coup_loads[q].start()

    barrier = pltpu.get_barrier_semaphore()
    for other in partners + [left, right]:
        pl.semaphore_signal(barrier, inc=1, device_id=(other,), device_id_type=MESH)

    for b in range(leaves):
        if b % 2 == 0:
            for load in loads[b // 2]:
                load.wait()
        local[0, b] = lax.dot_general(
            basis_in[pl.ds(b * rows, rows), :],
            fields[pl.ds((b + 1) * rows, rows), :],
            (((0,), (0,)), ((), ())),
            preferred_element_type=F32,
        ).astype(BF16)

    for q in range(local_bits, levels):
        coup_loads[q].start()
    for b in range(leaves):
        near_loads[b].start()
    basis_load.start()

    def mix(q, b, stacked):
        both = jnp.concatenate([coup[q, b, 0], coup[q, b, 1]], axis=1)
        return jnp.dot(both, stacked, preferred_element_type=F32).astype(BF16)

    copies = {}

    def send(level, b):
        copy = pltpu.make_async_remote_copy(
            src_ref=cross.at[level, b, sides[level]],
            dst_ref=cross.at[level, b, sides[level]],
            send_sem=send_sem.at[level, b],
            recv_sem=recv_sem.at[level, b],
            device_id=(partners[level],),
            device_id_type=MESH,
        )
        copy.start()
        copies[level, b] = copy

    for q in range(local_bits):
        coup_loads[q].wait()
        if q == local_bits - 1:
            pl.semaphore_wait(barrier, dev_bits + 2)
        stride = 1 << q
        for lo in range(leaves):
            if lo & stride:
                continue
            hi = lo | stride
            stacked = jnp.concatenate([local[q, lo], local[q, hi]], axis=0)
            for b in (lo, hi):
                mixed = mix(q, b, stacked)
                if q + 1 < local_bits:
                    local[q + 1, b] = mixed
                else:
                    cross[0, b, sides[0]] = mixed
                    send(0, b)

    to_left = pltpu.make_async_remote_copy(
        src_ref=fields.at[pl.ds(rows, rows)],
        dst_ref=fields.at[pl.ds((leaves + 1) * rows, rows)],
        send_sem=halo_send.at[0],
        recv_sem=halo_recv.at[0],
        device_id=(left,),
        device_id_type=MESH,
    )
    to_right = pltpu.make_async_remote_copy(
        src_ref=fields.at[pl.ds(leaves * rows, rows)],
        dst_ref=fields.at[pl.ds(0, rows)],
        send_sem=halo_send.at[1],
        recv_sem=halo_recv.at[1],
        device_id=(right,),
        device_id_type=MESH,
    )
    to_left.start()
    to_right.start()

    def near_field(b):
        near_loads[b].wait()
        if b == 0:
            to_right.wait_recv()
        if b == leaves - 1:
            to_left.wait_recv()
        total = None
        for j in range(3):
            block = fields[pl.ds((b + j) * rows, rows), :]
            if b == 0 and j == 0:
                block = jnp.where(me > 0, block, jnp.zeros_like(block))
            if b == leaves - 1 and j == 2:
                block = jnp.where(me < count - 1, block, jnp.zeros_like(block))
            term = jnp.dot(near[b, j], block, preferred_element_type=F32)
            total = term if total is None else total + term
        summed[b] = total

    first_leaves = [b for lo in range(leaves // 2) for b in (lo, lo + leaves // 2)]
    pending_near = list(range(1, leaves - 1)) + [0, leaves - 1]
    waited = set()
    stores = []
    clock = 0.0
    for when, level, slot in event_order(leaves, dev_bits):
        b = first_leaves[slot]
        while pending_near and when - clock > 0.4 and level > 0:
            near_field(pending_near.pop(0))
            clock += 0.4
        clock = max(clock, when)
        copies[level, b].wait_recv()
        q = local_bits + level
        if q not in waited:
            coup_loads[q].wait()
            waited.add(q)
        mixed = mix(q, b, cross[level, b].reshape(2 * rank, rank))
        if level + 1 < dev_bits:
            cross[level + 1, b, sides[level + 1]] = mixed
            send(level + 1, b)
            continue
        if not stores:
            basis_load.wait()
        while b in pending_near:
            near_field(pending_near.pop(0))
        far = jnp.dot(
            basis_out[pl.ds(b * rows, rows), :], mixed, preferred_element_type=F32
        )
        result[b] = (summed[b] + far).astype(BF16)
        store = pltpu.make_async_copy(
            result.at[b], result_hbm.at[pl.ds(b * rows, rows)], store_sem.at[b]
        )
        store.start()
        stores.append(store)

    for copy in copies.values():
        copy.wait_send()
    to_left.wait_send()
    to_right.wait_send()
    for store in stores:
        store.wait()


def per_device(fields, in_basis, out_basis, couplings, near_blocks):
    leaves, _, rows, _ = near_blocks.shape
    cols = fields.shape[1]
    rank = in_basis.shape[1]
    levels = couplings.shape[0]
    count = lax.axis_size("leaf")
    dev_bits = count.bit_length() - 1
    local_bits = levels - dev_bits
    dma = pltpu.SemaphoreType.DMA
    return pl.pallas_call(
        functools.partial(kernel, count),
        out_shape=jax.ShapeDtypeStruct(fields.shape, BF16),
        in_specs=[pl.BlockSpec(memory_space=pl.ANY)] * 5,
        out_specs=pl.BlockSpec(memory_space=pl.ANY),
        scratch_shapes=[
            pltpu.VMEM(((leaves + 2) * rows, cols), BF16),
            pltpu.VMEM((leaves * rows, rank), BF16),
            pltpu.VMEM((leaves * rows, rank), BF16),
            pltpu.VMEM(couplings.shape, BF16),
            pltpu.VMEM(near_blocks.shape, BF16),
            pltpu.VMEM((local_bits, leaves, rank, cols), BF16),
            pltpu.VMEM((dev_bits, leaves, 2, rank, cols), BF16),
            pltpu.VMEM((leaves, rank, cols), BF16),
            pltpu.VMEM((leaves, rows, cols), F32),
            pltpu.VMEM((leaves, rows, cols), BF16),
            dma((2, leaves // 2)),
            dma((levels,)),
            dma((leaves,)),
            dma,
            dma((leaves,)),
            dma((2,)),
            dma((2,)),
            dma((dev_bits, leaves)),
            dma((dev_bits, leaves)),
        ],
        compiler_params=pltpu.CompilerParams(
            collective_id=0, has_side_effects=True, vmem_limit_bytes=60 * 1024 * 1024
        ),
        name="butterfly",
    )(fields, in_basis, out_basis, couplings, near_blocks)


def solution(mesh):
    placed = (
        P("leaf", None),
        P("leaf", None),
        P("leaf", None),
        P(None, "leaf", None, None, None),
        P("leaf", None, None, None),
    )
    return jax.shard_map(
        per_device, mesh=mesh, in_specs=placed, out_specs=P("leaf", None), check_vma=False
    )
```

time: 106 us -> 71.1 us (0.67)
  Pallas kernels: 0 us -> 69.1 us
  waiting for transfers between devices: 42.8 us -> 0 us
  starting transfers between devices: 31.4 us -> 0 us
  matrix products: 21.1 us -> 0 us
  local copies, waits for them, and re-layouts: 9.69 us -> 1.87 us
    pallas_call x0 -> x1, Pallas kernels: none -> 69.1 us  [per_device(): pl.pallas_call(functools.partial(kernel, count), out_shape=jax.ShapeDtype...]
    ppermute x10 -> x0, waiting for transfers between devices: 42.8 us -> none  [the longest x8 42.8 us: from_partner(): return lax.ppermute(block, axis, route)]
    ppermute x10 -> x0, starting transfers between devices: 31.4 us -> none  [the longest x8 21.6 us: from_partner(): return lax.ppermute(block, axis, route)]
    dot_general x26 -> x0, matrix products: 21.1 us -> none  [the longest x15 12.3 us: cross_term(): jnp.einsum('bij,bjc->bic', chosen, coeffs, preferred_element_type=jnp.flo...]
    slice x2 -> x0, local copies, waits for them, and re-layouts: 5.9 us -> none  [the longest x1 5.89 us: per_device(): mixing = couplings[local_bits + step_bit]]
  transfers between devices with their start and end apart: 10 -> 0, of which waited for: 7 -> 0; matrix products, arithmetic and copies ran while one was open for 9% -> 0% of each run, Pallas kernels for 0% -> 0%
where the time goes in v1:
time: 71.1 us; the launch traced here: 71 us
  Pallas kernels  69.1 us (97%)
  local copies, waits for them, and re-layouts  1.87 us (3%)
    pallas_call x1, Pallas kernels, per_device(): pl.pallas_call(functools.partial(kernel, count), out_shape=jax.ShapeDtype...  69.1 us
    unnamed x1, local copies, waits for them, and re-layouts  1.87 us

profile of v1, /device:TPU:8, one launch (start us, length us, event | category | flops | bytes accessed | tf_op | source)
XLA Modules:
  0.0 71.0 jit_solution(10921764768597701527)
XLA Ops:
  0.0 69.1 %butterfly.1 = bf16[2048,128]{1,0:T(8,128)(2,1)} custom-call(bf16[2048,128]{1,0:T(8,128)(2,1)} %fields_hbm.1, bf16[2048,128]{1,0:T(8,128)(2,1)} %in_hbm.1, bf16[2048,128]{1,0:T(8,128)(2,1)} %out_hbm.1, bf16[11,8,2,128,128]{4,3,2,1,0:T(8,128)(2,1)} %coup_hbm.1, bf16[8,3,256,256]{3,2,1,0:T(8,128)(2,1)} %near_hbm.1), custom_call_target="tpu_custom_call" | custom-call | tf_op jit(solution)/shard_map/butterfly/pallas_call | solution.py:259
  69.1 1.9 %copy.7 = bf16[2048,128]{1,0:T(8,128)(2,1)} copy(bf16[2048,128]{1,0:T(8,128)(2,1)} %butterfly.1) | data formatting | bytes 1048576

commit v2 on v1

--- a/solution.py
+++ b/solution.py
@@ -17,9 +17,9 @@
         (0.9, 0.10, "c"),
         (1.7, 0.70, "x"),
         (2.4, 0.70, "x"),
-        (1.7, 0.35, "z"),
+        (1.7, 0.70, "z"),
         (2.4, 1.40, "z"),
-        (4.0, 1.40, "z"),
+        (4.0, 1.90, "z"),
         (1.7, 0.70, "y"),
         (2.4, 0.70, "y"),
     ]

time: 71.1 us -> 76.3 us (1.073)
  Pallas kernels: 69.1 us -> 74.2 us
    pallas_call x1, Pallas kernels: 69.1 us -> 74.2 us  [per_device(): pl.pallas_call(functools.partial(kernel, count), out_shape=jax.ShapeDtype...]
where the time goes in v2:
time: 76.3 us; the launch traced here: 76.1 us
  Pallas kernels  74.2 us (97%)
  local copies, waits for them, and re-layouts  1.87 us (2%)
    pallas_call x1, Pallas kernels, per_device(): pl.pallas_call(functools.partial(kernel, count), out_shape=jax.ShapeDtype...  74.2 us
    unnamed x1, local copies, waits for them, and re-layouts  1.87 us

profile of v2, /device:TPU:8, one launch (start us, length us, event | category | flops | bytes accessed | tf_op | source)
XLA Modules:
  0.0 76.1 jit_solution(16417194560964212751)
XLA Ops:
  0.0 74.2 %butterfly.1 = bf16[2048,128]{1,0:T(8,128)(2,1)} custom-call(bf16[2048,128]{1,0:T(8,128)(2,1)} %fields_hbm.1, bf16[2048,128]{1,0:T(8,128)(2,1)} %in_hbm.1, bf16[2048,128]{1,0:T(8,128)(2,1)} %out_hbm.1, bf16[11,8,2,128,128]{4,3,2,1,0:T(8,128)(2,1)} %coup_hbm.1, bf16[8,3,256,256]{3,2,1,0:T(8,128)(2,1)} %near_hbm.1), custom_call_target="tpu_custom_call" | custom-call | tf_op jit(solution)/shard_map/butterfly/pallas_call | solution.py:259
  74.2 1.9 %copy.7 = bf16[2048,128]{1,0:T(8,128)(2,1)} copy(bf16[2048,128]{1,0:T(8,128)(2,1)} %butterfly.1) | data formatting | bytes 1048576
